TPU v7x, 512 devices: a whole 4x4x16 slice. The times are simulated.
512 devices in a mesh: gauss: 128 (over z, x, core), view: 4 (over y).
Axes of the slice: x: 4, y: 4, z: 16, core: 2. Of those that a mesh axis runs over, the one named last changes fastest.
Arguments:
- params: bfloat16 [64, 131072], P(None, 'gauss'), may hold values from -5 to 2, as said below
- lists: int32 [2048, 128], P(('gauss', 'view')), may hold values from -1 to 131071, as said below
- tile_pos: int32 [2048], P(('gauss', 'view')), may hold values from 0 to 255
- cam_index: int32 [2048], P(('gauss', 'view')), may hold values from 0 to 15
- cams: float32 [28, 16], replicated, may hold values from -1 to 1100, as said below
- targets: float32 [3, 2048, 256], P(None, ('gauss', 'view')), may hold values from 0 to 1
Outputs:
- rendered: float32 [3, 2048, 256], P(None, ('gauss', 'view'))
- grads: float32 [64, 131072], P(None, 'gauss')
Inputs may be any that keep to these rules, and one draw needn't show every extreme that they name: `lists`: within each tile the entries that are not -1 come first. The entries of one device's 4 tiles that are not -1 name at most 4 times Gaussians of one gauss index (blocks of 1024 consecutive Gaussians), and in every draw some gauss index is named exactly 4 times by the tiles of every device; the number of entries that are not -1 differs from device to device. `cams`: columns are cameras: rows 0-8 a rotation matrix, 9-11 a translation putting every Gaussian mean at depth 2.4 or more, row 12 the focal length, rows 13-27 appearance weights. `params`: rows 6-9 are quaternions whose first component is 1 or more.
All inputs are finite; a program needn't handle non-finite values.
Results may differ from a plain program's by a relative error of at most 0.0003.
Values may be sent and summed in bfloat16 or wider, within the bound.
A program may use at most 64 MiB of HBM per device.

v0:
```python
import jax
import jax.numpy as jnp
from jax import lax
from jax.sharding import PartitionSpec as P

WIN = 16
HIGH = lax.Precision.HIGHEST


def sh_terms(dir_x, dir_y, dir_z):
    return [
        jnp.ones_like(dir_x),
        dir_x,
        dir_y,
        dir_z,
        dir_x * dir_y,
        dir_y * dir_z,
        dir_x * dir_z,
        dir_x * dir_x - dir_y * dir_y,
        3.0 * dir_z * dir_z - 1.0,
        dir_x * (dir_x * dir_x - 3.0 * dir_y * dir_y),
        dir_x * dir_y * dir_z,
        dir_y * (3.0 * dir_x * dir_x - dir_y * dir_y),
        dir_z * (dir_x * dir_x - dir_y * dir_y),
        dir_x * (5.0 * dir_z * dir_z - 1.0),
        dir_y * (5.0 * dir_z * dir_z - 1.0),
        dir_z * (5.0 * dir_z * dir_z - 3.0),
    ]


def fix_rows(row_vals, is_live):
    return row_vals.at[6].set(jnp.where(is_live, row_vals[6], 1.0))


def project(row_vals, camcols):
    mean_x, mean_y, mean_z = (row_vals[0], row_vals[1], row_vals[2])
    cam_rot = [camcols[index] for index in range(9)]
    focal = camcols[12]
    cam_x = cam_rot[0] * mean_x + cam_rot[1] * mean_y + cam_rot[2] * mean_z + camcols[9]
    cam_y = cam_rot[3] * mean_x + cam_rot[4] * mean_y + cam_rot[5] * mean_z + camcols[10]
    cam_z = cam_rot[6] * mean_x + cam_rot[7] * mean_y + cam_rot[8] * mean_z + camcols[11]
    inv_z = 1.0 / cam_z
    quaternion = row_vals[6:10]
    q_norm = jnp.sqrt(jnp.sum(quaternion * quaternion, axis=0))
    unit_w = quaternion[0] / q_norm
    unit_x = quaternion[1] / q_norm
    unit_y = quaternion[2] / q_norm
    unit_z = quaternion[3] / q_norm
    rotation = [
        [
            1.0 - 2.0 * (unit_y * unit_y + unit_z * unit_z),
            2.0 * (unit_x * unit_y - unit_w * unit_z),
            2.0 * (unit_x * unit_z + unit_w * unit_y),
        ],
        [
            2.0 * (unit_x * unit_y + unit_w * unit_z),
            1.0 - 2.0 * (unit_x * unit_x + unit_z * unit_z),
            2.0 * (unit_y * unit_z - unit_w * unit_x),
        ],
        [
            2.0 * (unit_x * unit_z - unit_w * unit_y),
            2.0 * (unit_y * unit_z + unit_w * unit_x),
            1.0 - 2.0 * (unit_x * unit_x + unit_y * unit_y),
        ],
    ]
    mixed = [
        [
            cam_rot[3 * row_i] * rotation[0][col_k]
            + cam_rot[3 * row_i + 1] * rotation[1][col_k]
            + cam_rot[3 * row_i + 2] * rotation[2][col_k]
            for col_k in range(3)
        ]
        for row_i in range(3)
    ]
    jac_scale = focal * inv_z
    proj_u = [
        jac_scale * mixed[0][col_k] - jac_scale * cam_x * inv_z * mixed[2][col_k]
        for col_k in range(3)
    ]
    proj_v = [
        jac_scale * mixed[1][col_k] - jac_scale * cam_y * inv_z * mixed[2][col_k]
        for col_k in range(3)
    ]
    var_diag = jnp.exp(2.0 * row_vals[3:6])
    cov_a = (
        proj_u[0] * proj_u[0] * var_diag[0]
        + proj_u[1] * proj_u[1] * var_diag[1]
        + proj_u[2] * proj_u[2] * var_diag[2]
        + 0.3
    )
    cov_b = (
        proj_u[0] * proj_v[0] * var_diag[0]
        + proj_u[1] * proj_v[1] * var_diag[1]
        + proj_u[2] * proj_v[2] * var_diag[2]
    )
    cov_c = (
        proj_v[0] * proj_v[0] * var_diag[0]
        + proj_v[1] * proj_v[1] * var_diag[1]
        + proj_v[2] * proj_v[2] * var_diag[2]
        + 0.3
    )
    determinant = cov_a * cov_c - cov_b * cov_b
    opacity = jax.nn.sigmoid(row_vals[10])
    distance = jnp.sqrt(cam_x * cam_x + cam_y * cam_y + cam_z * cam_z)
    terms = sh_terms(cam_x / distance, cam_y / distance, cam_z / distance)
    colors = []
    for chan in range(3):
        shade = 0.5 + sum(
            (row_vals[11 + 16 * chan + basis_b] * terms[basis_b] for basis_b in range(16))
        )
        shade = shade + sum(
            (row_vals[59 + feat_j] * camcols[13 + 3 * feat_j + chan] for feat_j in range(5))
        )
        colors.append(shade)
    centre_u = focal * cam_x * inv_z
    centre_v = focal * cam_y * inv_z
    return jnp.stack(
        [
            centre_u,
            centre_v,
            cov_c / determinant,
            -cov_b / determinant,
            cov_a / determinant,
            opacity,
            colors[0],
            colors[1],
            colors[2],
        ]
    )


def render(attrs, is_live, pixel_x, pixel_y):
    diff_x = pixel_x[None, :] - attrs[0][:, None]
    diff_y = pixel_y[None, :] - attrs[1][:, None]
    power = -0.5 * (
        attrs[2][:, None] * diff_x * diff_x
        + 2.0 * attrs[3][:, None] * diff_x * diff_y
        + attrs[4][:, None] * diff_y * diff_y
    )
    alpha = jnp.where(is_live[:, None], attrs[5][:, None] * jnp.exp(power), 0.0)
    keeping = jnp.cumprod(1.0 - alpha, axis=0)
    transmit = jnp.concatenate([jnp.ones((1, alpha.shape[1]), alpha.dtype), keeping[:-1]], axis=0)
    return jnp.dot(attrs[6:9], alpha * transmit, precision=HIGH)


def pixels(position):
    pixel_idx = jnp.arange(256)
    pixel_x = (16 * (position % WIN - WIN // 2) + pixel_idx % 16).astype(jnp.float32) + 0.5
    pixel_y = (16 * (position // WIN - WIN // 2) + pixel_idx // 16).astype(jnp.float32) + 0.5
    return (pixel_x, pixel_y)


def tile_grads(row_vals, camcol, is_live, pixel_x, pixel_y, target):

    def loss_of(params_in):
        picture = render(project(params_in, camcol[:, None]), is_live, pixel_x, pixel_y)
        return (0.5 * jnp.sum((picture - target) ** 2), picture)

    loss_val, pullback, picture = jax.vjp(loss_of, row_vals, has_aux=True)
    return (picture, pullback(jnp.ones_like(loss_val))[0])


def camera_columns(cams, camera_ids):
    selector = (camera_ids[None, :] == jnp.arange(cams.shape[1])[:, None]).astype(jnp.float32)
    return jnp.dot(cams, selector, precision=HIGH)


def one_tile(rows_in, live_in, camcol, pos_x, pos_y, target):
    return tile_grads(
        fix_rows(rows_in.astype(jnp.float32), live_in), camcol, live_in, pos_x, pos_y, target
    )


def on_device(params, lists, tile_pos, cam_index, cams, targets):
    owners = lax.axis_size("gauss")
    g_dev = params.shape[1]
    width = params.shape[0]
    n_tiles, list_len = lists.shape
    capacity = n_tiles * list_len // owners
    flat_ids = lists.reshape(-1)
    is_live = flat_ids >= 0
    owner_idx = jnp.where(is_live, flat_ids // g_dev, owners)
    selector = (owner_idx[:, None] == jnp.arange(owners)[None, :]).astype(jnp.int32)
    ranks = jnp.sum((jnp.cumsum(selector, axis=0) - selector) * selector, axis=1)
    slot_pos = jnp.where(is_live, owner_idx * capacity + ranks, owners * capacity)
    read_pos = jnp.minimum(slot_pos, owners * capacity - 1)
    local_idx = jnp.where(is_live, flat_ids % g_dev, -1)
    tile_cams = camera_columns(cams, cam_index)
    pixel_x, pixel_y = jax.vmap(pixels)(tile_pos)
    tile_live = is_live.reshape(n_tiles, list_len)
    wanted = (
        jnp.full((owners * capacity,), -1, jnp.int32)
        .at[slot_pos]
        .set(local_idx, mode="drop")
        .reshape(owners, capacity)
    )
    received = lax.all_to_all(wanted, "gauss", split_axis=0, concat_axis=0, tiled=True).reshape(-1)
    received_live = received >= 0
    picked = jnp.take(params, jnp.maximum(received, 0), axis=1)
    returned = lax.all_to_all(
        picked.reshape(width, owners, capacity), "gauss", split_axis=1, concat_axis=1, tiled=True
    )
    slot_rows = jnp.take(returned.reshape(width, -1), read_pos, axis=1).reshape(
        width, n_tiles, list_len
    )
    pictures, tile_g = jax.vmap(one_tile, in_axes=(1, 0, 1, 0, 0, 1), out_axes=(1, 1))(
        slot_rows, tile_live, tile_cams, pixel_x, pixel_y, targets
    )
    slot_g = tile_g.reshape(width, -1)
    sent_g = (
        jnp.zeros((width, owners * capacity), jnp.float32).at[:, slot_pos].set(slot_g, mode="drop")
    )
    row_g = lax.all_to_all(
        sent_g.reshape(width, owners, capacity), "gauss", split_axis=1, concat_axis=1, tiled=True
    ).reshape(width, -1)
    targets_idx = jnp.where(received_live, received, g_dev)
    summed = jnp.zeros((width, g_dev), jnp.float32).at[:, targets_idx].add(row_g, mode="drop")
    grads = lax.psum(summed, "view")
    return (pictures, grads)


def solution(mesh):
    return jax.shard_map(
        on_device,
        mesh=mesh,
        in_specs=(
            P(None, "gauss"),
            P(("gauss", "view"), None),
            P(("gauss", "view")),
            P(("gauss", "view")),
            P(),
            P(None, ("gauss", "view"), None),
        ),
        out_specs=(P(None, ("gauss", "view"), None), P(None, "gauss")),
        check_vma=False,
    )
```

profile of v0, /device:TPU:2, one launch (start us, length us, event | category | flops | bytes accessed | tf_op | source)
XLA Modules:
  0.0 217.4 jit_solution(6644110838534625728)
XLA Ops:
  8.7 2.4 %scatter_custom_fusion = s32[512]{0:T(512)S(1)} fusion(s32[512]{0:T(512)S(1)} %bitcast.784, s32[512]{0:T(512)S(1)} %get-tuple-element.304, s32[]{:T(128)} %constant.170.clone.1), kind=kCustom, calls=%fused_computation.691 | custom fusion | bytes 2052 | tf_op jit(solution)/shard_map/scatter | solution.py:194
  11.9 19.6 %all-to-all-start = ((s32[128,1,4]{2,1,0:T(1,128)}), s32[128,1,4]{2,1,0:T(1,128)S(1)}, u32[]{:S(2)}, u32[]{:S(2)}) async-start(s32[128,1,4]{2,1,0:T(1,128)} %bitcast.8), calls=%async_computation | async-start | bytes 131072 | tf_op jit(solution)/shard_map/all_to_all | solution.py:197
  31.7 1.0 slice_reduce_fusion.15
  34.1 11.2 %all-to-all-done = s32[128,1,4]{2,1,0:T(1,128)S(1)} async-done(((s32[128,1,4]{2,1,0:T(1,128)}), s32[128,1,4]{2,1,0:T(1,128)S(1)}, u32[]{:S(2)}, u32[]{:S(2)}) %all-to-all-start) | async-done | bytes 2080 | tf_op jit(solution)/shard_map/all_to_all | solution.py:197
  47.6 1.3 gather_fusion
  49.9 6.6 %all-to-all-start.1 = ((bf16[128,2,128]{2,1,0:T(2,128)(2,1)}), bf16[128,2,128]{2,1,0:T(2,128)(2,1)S(1)}, u32[]{:S(2)}, u32[]{:S(2)}) async-start(bf16[128,2,128]{2,1,0:T(2,128)(2,1)} %reshape.12609), calls=%async_computation.1 | async-start | bytes 131072 | tf_op jit(solution)/shard_map/all_to_all | solution.py:200
  56.9 13.6 %all-to-all-done.1 = bf16[128,2,128]{2,1,0:T(2,128)(2,1)S(1)} async-done(((bf16[128,2,128]{2,1,0:T(2,128)(2,1)}), bf16[128,2,128]{2,1,0:T(2,128)(2,1)S(1)}, u32[]{:S(2)}, u32[]{:S(2)}) %all-to-all-start.1) | async-done | bytes 65568 | tf_op jit(solution)/shard_map/all_to_all | solution.py:200
  70.6 1.3 gather_fusion.1
  92.9 1.1 fusion.23
  94.0 1.8 fusion.22
  97.4 0.9 copy-done.12
  99.4 0.8 copy-done.2
  110.7 0.8 copy-done.20
  111.7 0.8 copy-done.9
  112.6 0.9 copy-done.7
  115.6 0.8 copy-done.17
  117.2 1.5 fusion.13
  121.9 0.9 multiply_multiply_fusion.26
  128.2 1.9 scatter_custom_fusion.1
  130.3 22.8 %all_to_all.19 = f32[128,1,256]{2,1,0:T(1,128)S(1)} all-to-all(f32[128,1,256]{2,1,0:T(1,128)S(1)} %reshape.12611), channel_id=1, replica_groups=mesh['gauss'=128,'view'=4] {'gauss'}, dimensions={0} | all-to-all | bytes 262144 | tf_op jit(solution)/shard_map/all_to_all | solution.py:213
  153.6 1.0 reduce.62
  154.7 3.2 %scatter_custom_fusion.2 = f32[64,1024]{0,1:T(8,128)} fusion(s32[512]{0:T(512)} %bitcast.783, f32[512,64]{1,0:T(8,128)S(1)} %bitcast.772, f32[]{:T(128)} %constant.184.clone.1), kind=kCustom, calls=%fused_computation.47 | custom fusion | flops 32768 | bytes 262656 | tf_op jit(solution)/shard_map/scatter-add | solution.py:217
  159.2 49.4 %all-reduce.139.cloned.1.call-done = f32[64,1024]{0,1:T(8,128)} async-done(((f32[64,1024]{0,1:T(8,128)}), f32[64,1024]{0,1:T(8,128)}) %all-reduce.139.cloned.1.call-update) | async-done | bytes 262160 | tf_op jit(solution)/shard_map/psum | solution.py:218
  208.6 1.9 copy.288
  (612 shorter events, 52.8 us)
Async XLA Ops:
  7.9 67.9 %copy-start.94 = (pred[4,128]{1,0:T(4,128)(4,1)}, pred[4,128]{1,0:T(4,128)(4,1)S(1)}, u32[]{:S(2)}) copy-start(pred[4,128]{1,0:T(4,128)(4,1)S(1)} %get-tuple-element.152) | copy-start | bytes 1540
  11.9 33.5 %all-to-all-start = ((s32[128,1,4]{2,1,0:T(1,128)}), s32[128,1,4]{2,1,0:T(1,128)S(1)}, u32[]{:S(2)}, u32[]{:S(2)}) async-start(s32[128,1,4]{2,1,0:T(1,128)} %bitcast.8), calls=%async_computation | async-start | bytes 131072 | tf_op jit(solution)/shard_map/all_to_all | solution.py:197
  32.7 41.5 %copy-start.56 = (f32[4]{0:T(128)}, f32[4]{0:T(128)S(1)}, u32[]{:S(2)}) copy-start(f32[4]{0:T(128)S(1)} %get-tuple-element.47) | copy-start | bytes 52
  32.7 41.5 %copy-start.63 = (f32[4]{0:T(128)}, f32[4]{0:T(128)S(1)}, u32[]{:S(2)}) copy-start(f32[4]{0:T(128)S(1)} %get-tuple-element.48) | copy-start | bytes 52
  32.7 41.5 %copy-start.138 = (f32[4]{0:T(128)}, f32[4]{0:T(128)S(1)}, u32[]{:S(2)}) copy-start(f32[4]{0:T(128)S(1)} %get-tuple-element.46) | copy-start | bytes 52
  32.7 42.5 %copy-start.85 = (f32[4]{0:T(128)}, f32[4]{0:T(128)S(1)}, u32[]{:S(2)}) copy-start(f32[4]{0:T(128)S(1)} %get-tuple-element.31) | copy-start | bytes 52
  33.0 41.2 %copy-start.58 = (f32[4]{0:T(128)}, f32[4]{0:T(128)S(1)}, u32[]{:S(2)}) copy-start(f32[4]{0:T(128)S(1)} %get-tuple-element.55) | copy-start | bytes 52
  33.0 41.2 %copy-start.61 = (f32[4]{0:T(128)}, f32[4]{0:T(128)S(1)}, u32[]{:S(2)}) copy-start(f32[4]{0:T(128)S(1)} %get-tuple-element.51) | copy-start | bytes 52
  33.0 41.2 %copy-start.65 = (f32[4]{0:T(128)}, f32[4]{0:T(128)S(1)}, u32[]{:S(2)}) copy-start(f32[4]{0:T(128)S(1)} %get-tuple-element.56) | copy-start | bytes 52
  33.0 41.2 %copy-start.68 = (f32[4]{0:T(128)}, f32[4]{0:T(128)S(1)}, u32[]{:S(2)}) copy-start(f32[4]{0:T(128)S(1)} %get-tuple-element.57) | copy-start | bytes 52
  33.1 41.2 %copy-start.71 = (f32[4]{0:T(128)}, f32[4]{0:T(128)S(1)}, u32[]{:S(2)}) copy-start(f32[4]{0:T(128)S(1)} %get-tuple-element.50) | copy-start | bytes 52
  33.1 41.2 %copy-start.73 = (f32[4]{0:T(128)}, f32[4]{0:T(128)S(1)}, u32[]{:S(2)}) copy-start(f32[4]{0:T(128)S(1)} %get-tuple-element.53) | copy-start | bytes 52
  33.1 41.2 %copy-start.83 = (f32[4]{0:T(128)}, f32[4]{0:T(128)S(1)}, u32[]{:S(2)}) copy-start(f32[4]{0:T(128)S(1)} %get-tuple-element.52) | copy-start | bytes 52
  33.1 41.2 %copy-start.140 = (f32[4]{0:T(128)}, f32[4]{0:T(128)S(1)}, u32[]{:S(2)}) copy-start(f32[4]{0:T(128)S(1)} %get-tuple-element.54) | copy-start | bytes 52
  33.1 41.2 %copy-start.143 = (f32[4]{0:T(128)}, f32[4]{0:T(128)S(1)}, u32[]{:S(2)}) copy-start(f32[4]{0:T(128)S(1)} %get-tuple-element.49) | copy-start | bytes 52
  33.8 40.5 %copy-start.196 = (f32[4]{0:T(128)}, f32[4]{0:T(128)S(1)}, u32[]{:S(2)}) copy-start(f32[4]{0:T(128)S(1)} %broadcast_multiply_fusion.24) | copy-start | bytes 52
  33.8 40.4 %copy-start.185 = (f32[4]{0:T(128)}, f32[4]{0:T(128)S(1)}, u32[]{:S(2)}) copy-start(f32[4]{0:T(128)S(1)} %get-tuple-element.308) | copy-start | bytes 52
  33.8 40.4 %copy-start.187 = (f32[4]{0:T(128)}, f32[4]{0:T(128)S(1)}, u32[]{:S(2)}) copy-start(f32[4]{0:T(128)S(1)} %get-tuple-element.309) | copy-start | bytes 52
  33.9 40.4 %copy-start.189 = (f32[4]{0:T(128)}, f32[4]{0:T(128)S(1)}, u32[]{:S(2)}) copy-start(f32[4]{0:T(128)S(1)} %get-tuple-element.310) | copy-start | bytes 52
  33.9 40.4 %copy-start.191 = (f32[4]{0:T(128)}, f32[4]{0:T(128)S(1)}, u32[]{:S(2)}) copy-start(f32[4]{0:T(128)S(1)} %get-tuple-element.311) | copy-start | bytes 52
  33.9 40.4 %copy-start.192 = (f32[4]{0:T(128)}, f32[4]{0:T(128)S(1)}, u32[]{:S(2)}) copy-start(f32[4]{0:T(128)S(1)} %get-tuple-element.312) | copy-start | bytes 52
  33.9 40.4 %copy-start.193 = (f32[4]{0:T(128)}, f32[4]{0:T(128)S(1)}, u32[]{:S(2)}) copy-start(f32[4]{0:T(128)S(1)} %get-tuple-element.313) | copy-start | bytes 52
  49.9 20.6 %all-to-all-start.1 = ((bf16[128,2,128]{2,1,0:T(2,128)(2,1)}), bf16[128,2,128]{2,1,0:T(2,128)(2,1)S(1)}, u32[]{:S(2)}, u32[]{:S(2)}) async-start(bf16[128,2,128]{2,1,0:T(2,128)(2,1)} %reshape.12609), calls=%async_computation.1 | async-start | bytes 131072 | tf_op jit(solution)/shard_map/all_to_all | solution.py:200
  56.6 152.0 %all-reduce.139.cloned.1.call-start = ((), (), s32[]{:S(2)}) async-start(), calls=%async_computation.3 | async-start | bytes 1048576 | tf_op jit(solution)/shard_map/psum | solution.py:218
  (183 other events, 386.3 us)
Sparse Core Ops, SparseCore 0:
  158.0 50.5 all-reduce.138
where the time goes:
time: 219 us; the launch traced here: 217 us
  waiting for transfers between devices  74.3 us (34%)
  local copies, waits for them, and re-layouts  54.9 us (25%)
  starting transfers between devices  26.4 us (12%)
  blocking collectives  22.8 us (10%)
  other arithmetic  18.4 us (8%)
  between operations  16.9 us (8%)
  matrix products  3.73 us (2%)
    psum x1, waiting for transfers between devices, on_device(): grads = lax.psum(summed, 'view')  49.4 us
    unnamed x411, local copies, waits for them, and re-layouts  38.7 us
    all_to_all x1, blocking collectives, on_device(): lax.all_to_all(sent_g.reshape(width, owners, capacity), 'gauss', split_ax...  22.8 us
    all_to_all x1, starting transfers between devices, on_device(): lax.all_to_all(wanted, 'gauss', split_axis=0, concat_axis=0, tiled=True)  19.6 us
    all_to_all x1, waiting for transfers between devices, on_device(): lax.all_to_all(picked.reshape(width, owners, capacity), 'gauss', split_ax...  13.6 us
    all_to_all x1, waiting for transfers between devices, on_device(): lax.all_to_all(wanted, 'gauss', split_axis=0, concat_axis=0, tiled=True)  11.2 us
    all_to_all x1, starting transfers between devices, on_device(): lax.all_to_all(picked.reshape(width, owners, capacity), 'gauss', split_ax...  6.64 us
  transfers between devices with their start and end apart: 3, of which 3 were waited for; matrix products, arithmetic and copies ran while one was open for 1% of the time, Pallas kernels for 0%

commit v1 on v0

--- a/solution.py
+++ b/solution.py
@@ -215,7 +215,7 @@
     ).reshape(width, -1)
     targets_idx = jnp.where(received_live, received, g_dev)
     summed = jnp.zeros((width, g_dev), jnp.float32).at[:, targets_idx].add(row_g, mode="drop")
-    grads = lax.psum(summed, "view")
+    grads = jnp.sum(lax.all_gather(summed, "view"), axis=0)
     return (pictures, grads)
 
 

time: 219 us -> 193 us (0.88)
  waiting for transfers between devices: 74.3 us -> 47.6 us
    psum x1 -> x0, waiting for transfers between devices: 49.4 us -> none  [on_device(): grads = lax.psum(summed, 'view')]
    all_gather x0 -> x1, waiting for transfers between devices: none -> 22.7 us  [on_device(): grads = jnp.sum(lax.all_gather(summed, 'view'), axis=0)]
    unnamed x411 -> x410, local copies, waits for them, and re-layouts: 38.7 us -> 36.8 us
where the time goes in v1:
time: 193 us; the launch traced here: 191 us
  local copies, waits for them, and re-layouts  53.9 us (28%)
  waiting for transfers between devices  47.6 us (25%)
  starting transfers between devices  26.4 us (14%)
  blocking collectives  22.8 us (12%)
  other arithmetic  19.7 us (10%)
  between operations  16.9 us (9%)
  matrix products  3.73 us (2%)
    unnamed x410, local copies, waits for them, and re-layouts  36.8 us
    all_to_all x1, blocking collectives, on_device(): lax.all_to_all(sent_g.reshape(width, owners, capacity), 'gauss', split_ax...  22.8 us
    all_gather x1, waiting for transfers between devices, on_device(): grads = jnp.sum(lax.all_gather(summed, 'view'), axis=0)  22.7 us
    all_to_all x1, starting transfers between devices, on_device(): lax.all_to_all(wanted, 'gauss', split_axis=0, concat_axis=0, tiled=True)  19.6 us
    all_to_all x1, waiting for transfers between devices, on_device(): lax.all_to_all(picked.reshape(width, owners, capacity), 'gauss', split_ax...  13.6 us
    all_to_all x1, waiting for transfers between devices, on_device(): lax.all_to_all(wanted, 'gauss', split_axis=0, concat_axis=0, tiled=True)  11.2 us
    all_to_all x1, starting transfers between devices, on_device(): lax.all_to_all(picked.reshape(width, owners, capacity), 'gauss', split_ax...  6.64 us
  transfers between devices with their start and end apart: 3, of which 3 were waited for; matrix products, arithmetic and copies ran while one was open for 1% of the time, Pallas kernels for 0%

profile of v1, /device:TPU:2, one launch (start us, length us, event | category | flops | bytes accessed | tf_op | source)
XLA Modules:
  0.0 191.0 jit_solution(193808470100192962)
XLA Ops:
  8.7 2.4 %scatter_custom_fusion = s32[512]{0:T(512)S(1)} fusion(s32[512]{0:T(512)S(1)} %bitcast.786, s32[512]{0:T(512)S(1)} %get-tuple-element.304, s32[]{:T(128)} %constant.170.clone.1), kind=kCustom, calls=%fused_computation.691 | custom fusion | bytes 2052 | tf_op jit(solution)/shard_map/scatter | solution.py:194
  11.9 19.6 %all-to-all-start = ((s32[128,1,4]{2,1,0:T(1,128)}), s32[128,1,4]{2,1,0:T(1,128)S(1)}, u32[]{:S(2)}, u32[]{:S(2)}) async-start(s32[128,1,4]{2,1,0:T(1,128)} %bitcast.8), calls=%async_computation | async-start | bytes 131072 | tf_op jit(solution)/shard_map/all_to_all | solution.py:197
  31.7 1.0 slice_reduce_fusion.15
  34.1 11.2 %all-to-all-done = s32[128,1,4]{2,1,0:T(1,128)S(1)} async-done(((s32[128,1,4]{2,1,0:T(1,128)}), s32[128,1,4]{2,1,0:T(1,128)S(1)}, u32[]{:S(2)}, u32[]{:S(2)}) %all-to-all-start) | async-done | bytes 2080 | tf_op jit(solution)/shard_map/all_to_all | solution.py:197
  47.6 1.3 gather_fusion
  49.9 6.6 %all-to-all-start.1 = ((bf16[128,2,128]{2,1,0:T(2,128)(2,1)}), bf16[128,2,128]{2,1,0:T(2,128)(2,1)S(1)}, u32[]{:S(2)}, u32[]{:S(2)}) async-start(bf16[128,2,128]{2,1,0:T(2,128)(2,1)} %reshape.12610), calls=%async_computation.1 | async-start | bytes 131072 | tf_op jit(solution)/shard_map/all_to_all | solution.py:200
  56.9 13.6 %all-to-all-done.1 = bf16[128,2,128]{2,1,0:T(2,128)(2,1)S(1)} async-done(((bf16[128,2,128]{2,1,0:T(2,128)(2,1)}), bf16[128,2,128]{2,1,0:T(2,128)(2,1)S(1)}, u32[]{:S(2)}, u32[]{:S(2)}) %all-to-all-start.1) | async-done | bytes 65568 | tf_op jit(solution)/shard_map/all_to_all | solution.py:200
  70.6 1.3 gather_fusion.1
  92.9 1.1 fusion.23
  94.0 1.8 fusion.22
  97.4 0.9 copy-done.12
  99.4 0.8 copy-done.2
  111.7 0.8 copy-done.9
  112.6 0.9 copy-done.7
  115.6 0.8 copy-done.17
  117.2 1.5 fusion.13
  121.9 0.9 multiply_multiply_fusion.26
  128.2 1.9 scatter_custom_fusion.1
  130.3 22.8 %all_to_all.19 = f32[128,1,256]{2,1,0:T(1,128)S(1)} all-to-all(f32[128,1,256]{2,1,0:T(1,128)S(1)} %reshape.12612), channel_id=1, replica_groups=mesh['gauss'=128,'view'=4] {'gauss'}, dimensions={0} | all-to-all | bytes 262144 | tf_op jit(solution)/shard_map/all_to_all | solution.py:213
  153.6 1.0 reduce.62
  154.7 2.5 %scatter_custom_fusion.2 = f32[64,1024]{0,1:T(8,128)S(1)} fusion(s32[512]{0:T(512)} %bitcast.785, f32[512,64]{1,0:T(8,128)S(1)} %bitcast.774, f32[]{:T(128)} %constant.184.clone.1), kind=kCustom, calls=%fused_computation.47 | custom fusion | flops 32768 | bytes 262656 | tf_op jit(solution)/shard_map/scatter-add | solution.py:217
  157.2 0.9 copy.286
  159.4 22.7 %all-gather.3.cloned.1.call-done = f32[256,1024]{1,0:T(8,128)} async-done(((f32[64,1024]{1,0:T(8,128)}), f32[256,1024]{1,0:T(8,128)}) %all-gather.3.cloned.1.call-update) | async-done | bytes 1048592 | tf_op jit(solution)/shard_map/all_gather | solution.py:218
  182.1 2.0 %reduce_sum.104 = f32[64,1024]{1,0:T(8,128)} reduce(f32[4,64,1024]{2,1,0:T(8,128)} %bitcast.769, f32[]{:T(128)} %constant.184.clone.1), dimensions={0}, to_apply=%region_13.14 | reduce | flops 196608 | bytes 1310724 | tf_op jit(solution)/shard_map/reduce_sum | solution.py:218
  (613 shorter events, 53.6 us)
Async XLA Ops:
  7.9 67.9 %copy-start.94 = (pred[4,128]{1,0:T(4,128)(4,1)}, pred[4,128]{1,0:T(4,128)(4,1)S(1)}, u32[]{:S(2)}) copy-start(pred[4,128]{1,0:T(4,128)(4,1)S(1)} %get-tuple-element.152) | copy-start | bytes 1540
  11.9 33.5 %all-to-all-start = ((s32[128,1,4]{2,1,0:T(1,128)}), s32[128,1,4]{2,1,0:T(1,128)S(1)}, u32[]{:S(2)}, u32[]{:S(2)}) async-start(s32[128,1,4]{2,1,0:T(1,128)} %bitcast.8), calls=%async_computation | async-start | bytes 131072 | tf_op jit(solution)/shard_map/all_to_all | solution.py:197
  32.7 41.5 %copy-start.56 = (f32[4]{0:T(128)}, f32[4]{0:T(128)S(1)}, u32[]{:S(2)}) copy-start(f32[4]{0:T(128)S(1)} %get-tuple-element.47) | copy-start | bytes 52
  32.7 41.5 %copy-start.63 = (f32[4]{0:T(128)}, f32[4]{0:T(128)S(1)}, u32[]{:S(2)}) copy-start(f32[4]{0:T(128)S(1)} %get-tuple-element.48) | copy-start | bytes 52
  32.7 41.5 %copy-start.138 = (f32[4]{0:T(128)}, f32[4]{0:T(128)S(1)}, u32[]{:S(2)}) copy-start(f32[4]{0:T(128)S(1)} %get-tuple-element.46) | copy-start | bytes 52
  32.7 42.5 %copy-start.85 = (f32[4]{0:T(128)}, f32[4]{0:T(128)S(1)}, u32[]{:S(2)}) copy-start(f32[4]{0:T(128)S(1)} %get-tuple-element.31) | copy-start | bytes 52
  33.0 41.2 %copy-start.58 = (f32[4]{0:T(128)}, f32[4]{0:T(128)S(1)}, u32[]{:S(2)}) copy-start(f32[4]{0:T(128)S(1)} %get-tuple-element.55) | copy-start | bytes 52
  33.0 41.2 %copy-start.61 = (f32[4]{0:T(128)}, f32[4]{0:T(128)S(1)}, u32[]{:S(2)}) copy-start(f32[4]{0:T(128)S(1)} %get-tuple-element.51) | copy-start | bytes 52
  33.0 41.2 %copy-start.65 = (f32[4]{0:T(128)}, f32[4]{0:T(128)S(1)}, u32[]{:S(2)}) copy-start(f32[4]{0:T(128)S(1)} %get-tuple-element.56) | copy-start | bytes 52
  33.0 41.2 %copy-start.68 = (f32[4]{0:T(128)}, f32[4]{0:T(128)S(1)}, u32[]{:S(2)}) copy-start(f32[4]{0:T(128)S(1)} %get-tuple-element.57) | copy-start | bytes 52
  33.1 41.2 %copy-start.71 = (f32[4]{0:T(128)}, f32[4]{0:T(128)S(1)}, u32[]{:S(2)}) copy-start(f32[4]{0:T(128)S(1)} %get-tuple-element.50) | copy-start | bytes 52
  33.1 41.2 %copy-start.73 = (f32[4]{0:T(128)}, f32[4]{0:T(128)S(1)}, u32[]{:S(2)}) copy-start(f32[4]{0:T(128)S(1)} %get-tuple-element.53) | copy-start | bytes 52
  33.1 41.2 %copy-start.83 = (f32[4]{0:T(128)}, f32[4]{0:T(128)S(1)}, u32[]{:S(2)}) copy-start(f32[4]{0:T(128)S(1)} %get-tuple-element.52) | copy-start | bytes 52
  33.1 41.2 %copy-start.140 = (f32[4]{0:T(128)}, f32[4]{0:T(128)S(1)}, u32[]{:S(2)}) copy-start(f32[4]{0:T(128)S(1)} %get-tuple-element.54) | copy-start | bytes 52
  33.1 41.2 %copy-start.143 = (f32[4]{0:T(128)}, f32[4]{0:T(128)S(1)}, u32[]{:S(2)}) copy-start(f32[4]{0:T(128)S(1)} %get-tuple-element.49) | copy-start | bytes 52
  33.8 40.5 %copy-start.196 = (f32[4]{0:T(128)}, f32[4]{0:T(128)S(1)}, u32[]{:S(2)}) copy-start(f32[4]{0:T(128)S(1)} %broadcast_multiply_fusion.24) | copy-start | bytes 52
  33.8 40.4 %copy-start.185 = (f32[4]{0:T(128)}, f32[4]{0:T(128)S(1)}, u32[]{:S(2)}) copy-start(f32[4]{0:T(128)S(1)} %get-tuple-element.308) | copy-start | bytes 52
  33.8 40.4 %copy-start.187 = (f32[4]{0:T(128)}, f32[4]{0:T(128)S(1)}, u32[]{:S(2)}) copy-start(f32[4]{0:T(128)S(1)} %get-tuple-element.309) | copy-start | bytes 52
  33.9 40.4 %copy-start.189 = (f32[4]{0:T(128)}, f32[4]{0:T(128)S(1)}, u32[]{:S(2)}) copy-start(f32[4]{0:T(128)S(1)} %get-tuple-element.310) | copy-start | bytes 52
  33.9 40.4 %copy-start.191 = (f32[4]{0:T(128)}, f32[4]{0:T(128)S(1)}, u32[]{:S(2)}) copy-start(f32[4]{0:T(128)S(1)} %get-tuple-element.311) | copy-start | bytes 52
  33.9 40.4 %copy-start.192 = (f32[4]{0:T(128)}, f32[4]{0:T(128)S(1)}, u32[]{:S(2)}) copy-start(f32[4]{0:T(128)S(1)} %get-tuple-element.312) | copy-start | bytes 52
  33.9 40.4 %copy-start.193 = (f32[4]{0:T(128)}, f32[4]{0:T(128)S(1)}, u32[]{:S(2)}) copy-start(f32[4]{0:T(128)S(1)} %get-tuple-element.313) | copy-start | bytes 52
  49.9 20.6 %all-to-all-start.1 = ((bf16[128,2,128]{2,1,0:T(2,128)(2,1)}), bf16[128,2,128]{2,1,0:T(2,128)(2,1)S(1)}, u32[]{:S(2)}, u32[]{:S(2)}) async-start(bf16[128,2,128]{2,1,0:T(2,128)(2,1)} %reshape.12610), calls=%async_computation.1 | async-start | bytes 131072 | tf_op jit(solution)/shard_map/all_to_all | solution.py:200
  56.6 125.6 %all-gather.3.cloned.1.call-start = ((), (), s32[]{:S(2)}) async-start(), calls=%async_computation.3 | async-start | bytes 1310720 | tf_op jit(solution)/shard_map/all_gather | solution.py:218
  (183 other events, 386.3 us)
Sparse Core Ops, SparseCore 0:
  158.2 23.8 all-gather.2
